TPU v7x, 32 devices: a whole 2x2x4 slice. The times are simulated.
32 devices in a mesh: groups: 2 (over x), row: 16 (over z, y, core).
Axes of the slice: x: 2, y: 2, z: 4, core: 2. Of those that a mesh axis runs over, the one named last changes fastest.
Arguments:
- pair_rows: bfloat16 [256, 128, 128], P(('groups', 'row')), parts along dimension 0, may hold values from -6 to 6
- in_gain: float32 [128], replicated, may hold values from 0.1 to 1.9
- w_left: bfloat16 [128, 128], replicated, may hold values from -0.5 to 0.5
- w_left_gate: bfloat16 [128, 128], replicated, may hold values from -0.5 to 0.5
- w_right: bfloat16 [128, 128], replicated, may hold values from -0.5 to 0.5
- w_right_gate: bfloat16 [128, 128], replicated, may hold values from -0.5 to 0.5
- w_gate: bfloat16 [128, 128], replicated, may hold values from -0.5 to 0.5
- w_out: bfloat16 [128, 128], replicated, may hold values from -0.5 to 0.5
- out_gain: float32 [128], replicated, may hold values from 0.1 to 1.9
- valid_len: int32 [2], P('groups'), parts along dimension 0, may hold values from 64 to 128
- window: int32 [2], P('groups'), parts along dimension 0, may hold values from 0 to 7
Outputs:
- update: bfloat16 [256, 16, 128], P(('groups', 'row')), parts along dimension 0
There are 2 independent parts, one for each index of `groups`. A program takes and returns all parts, laid end to end along the dimension named above; an argument that names none is the same for every part. Nothing has to cross between parts.
All inputs are finite; a program needn't handle non-finite values.
Results may differ from a plain program's by a relative error of at most 0.0078.
Values may be sent and summed in bfloat16 or wider, within the bound.
A program may use at most 128 MiB of HBM per device.

v0:
```python
import functools

import jax
import jax.numpy as jnp
from jax import lax
from jax.experimental import pallas as pl
from jax.experimental.pallas import tpu as pltpu
from jax.sharding import PartitionSpec as P


def layer_norm(values, gain):
    mean_v = jnp.mean(values, axis=-1, keepdims=True)
    centered = values - mean_v
    variance_v = jnp.mean(centered * centered, axis=-1, keepdims=True)
    return centered * lax.rsqrt(variance_v + 1e-05) * gain


def on_device(
    pair_rows,
    in_gain,
    w_left,
    w_left_gate,
    w_right,
    w_right_gate,
    w_gate,
    w_out,
    out_gain,
    valid_len,
    window,
):
    my_index = lax.axis_index("row")
    local_rows, tokens_all, channels = pair_rows.shape
    width_win = tokens_all // 8
    valid_upto = valid_len[0]
    start_block = window[0]
    start_row = start_block * width_win
    row_ids = my_index * local_rows + jnp.arange(local_rows, dtype=jnp.int32)
    row_live = (row_ids < valid_upto).astype(jnp.float32)
    col_live = (jnp.arange(tokens_all, dtype=jnp.int32) < valid_upto).astype(jnp.float32)
    live_mask = (row_live[:, None] * col_live[None, :])[:, :, None]
    normed = layer_norm(pair_rows.astype(jnp.float32), in_gain).astype(jnp.bfloat16)
    flat_rows = normed.reshape(-1, channels)
    joined = jnp.concatenate([w_left, w_left_gate, w_right, w_right_gate], axis=1)
    projected = jnp.dot(flat_rows, joined, preferred_element_type=jnp.float32)
    projected = projected.reshape(local_rows, tokens_all, 4 * channels)
    left_edge = (
        jax.nn.sigmoid(projected[:, :, channels : 2 * channels])
        * projected[:, :, :channels]
        * live_mask
    ).astype(jnp.bfloat16)
    right_edge = (
        jax.nn.sigmoid(projected[:, :, 3 * channels :])
        * projected[:, :, 2 * channels : 3 * channels]
        * live_mask
    ).astype(jnp.bfloat16)
    gate_in = lax.dynamic_slice_in_dim(normed, start_row, width_win, 1)
    gate_vals = jax.nn.sigmoid(
        jnp.dot(gate_in.reshape(-1, channels), w_gate, preferred_element_type=jnp.float32)
    )
    gate_vals = gate_vals.reshape(local_rows, width_win, channels)
    regrouped = lax.all_to_all(right_edge, "row", split_axis=1, concat_axis=0, tiled=True)
    picked = lax.dynamic_slice_in_dim(regrouped, start_row, width_win, 0)
    window_right = lax.all_gather(picked, "row", axis=1, tiled=True)
    product = jnp.einsum(
        "ikc,jkc->ijc", left_edge, window_right, preferred_element_type=jnp.float32
    )
    normed_out = layer_norm(product, out_gain).astype(jnp.bfloat16)
    result = jnp.dot(normed_out.reshape(-1, channels), w_out, preferred_element_type=jnp.float32)
    return (gate_vals * result.reshape(local_rows, width_win, channels)).astype(jnp.bfloat16)


MESH = pl.DeviceIdType.MESH
CHUNKS = 2
QUAD = 4
QUARTER, CROSS, GATHER, SWAP = 0, 3, 4, 7


def fused_kernel(
    valid_ref,
    window_ref,
    x_hbm,
    in_gain_hbm,
    w_left_hbm,
    w_left_gate_hbm,
    w_right_hbm,
    w_right_gate_hbm,
    w_gate_hbm,
    w_out_hbm,
    out_gain_hbm,
    o_ref,
    x_ref,
    in_gain_ref,
    w_left_ref,
    w_left_gate_ref,
    w_right_ref,
    w_right_gate_ref,
    w_gate_ref,
    w_out_ref,
    out_gain_ref,
    normed_ref,
    left_ref,
    parts,
    best,
    cross,
    win_ref,
    prod_ref,
    send_sem,
    recv_sem,
    load_sem,
):
    local_rows, tokens, channels = x_ref.shape
    depth = tokens // QUAD
    width = o_ref.shape[1]
    step = local_rows // CHUNKS

    me = lax.axis_index("row")
    core = lax.rem(me, 2)
    chip = lax.div(me, 2)
    quad = lax.div(chip, QUAD)
    spot = lax.rem(chip, QUAD)
    y = lax.rem(spot, 2)
    z = lax.div(spot, 2)
    spots = ((1 - z) * 2 + 1 - y, (1 - z) * 2 + y, z * 2 + 1 - y)

    def at(quad_, spot_, core_):
        return {"row": (quad_ * QUAD + spot_) * 2 + core_}

    peers = [at(quad, s, core) for s in spots]
    cross_peer = at(1 - quad, spot, core)
    core_peer = at(quad, spot, 1 - core)

    def quarter(s):
        return pl.ds(pl.multiple_of(s * depth, depth), depth)

    mine = quarter(spot)

    def copy(kind, q):
        rows = pl.ds(q * step, step)
        if kind < CROSS:
            src, dst, dev = x_ref.at[rows, quarter(spots[kind])], parts.at[kind, rows], peers[kind]
        elif kind == CROSS:
            src, dst, dev = best.at[rows], cross.at[rows], cross_peer
        elif kind < SWAP:
            src = dst = win_ref.at[core, rows, mine]
            dev = peers[kind - GATHER]
        else:
            src = dst = win_ref.at[core, rows]
            dev = core_peer
        return pltpu.make_async_remote_copy(
            src_ref=src,
            dst_ref=dst,
            send_sem=send_sem.at[kind, q],
            recv_sem=recv_sem.at[kind, q],
            device_id=dev,
            device_id_type=MESH,
        )

    barrier = pltpu.get_barrier_semaphore()
    everyone = peers + [cross_peer, core_peer]
    for peer in everyone:
        pl.semaphore_signal(barrier, inc=1, device_id=peer, device_id_type=MESH)
    loads = [
        pltpu.make_async_copy(src, dst, load_sem.at[n])
        for n, (src, dst) in enumerate(
            (
                *((x_hbm.at[pl.ds(q * step, step)], x_ref.at[pl.ds(q * step, step)]) for q in range(CHUNKS)),
                (in_gain_hbm, in_gain_ref),
                (w_left_hbm, w_left_ref),
                (w_left_gate_hbm, w_left_gate_ref),
                (w_gate_hbm, w_gate_ref),
                (w_right_hbm, w_right_ref),
                (w_right_gate_hbm, w_right_gate_ref),
                (w_out_hbm, w_out_ref),
                (out_gain_hbm, out_gain_ref),
            )
        )
    ]
    for load in loads:
        load.start()
    pl.semaphore_wait(barrier, len(everyone))
    for q in range(CHUNKS):
        loads[q].wait()
        for t in range(3):
            copy(QUARTER + t, q).start()
    for load in loads[CHUNKS:]:
        load.wait()

    win = window_ref[0]
    win_v = jnp.full((depth, channels), win, jnp.int32)

    def flag(cond):
        return jnp.where(cond, 1.0, 0.0).astype(jnp.bfloat16)

    owners = [flag(win_v == quad * QUAD + s) for s in spots]
    own_quad = flag(jnp.logical_and(win_v >= quad * QUAD, win_v < (quad + 1) * QUAD))

    def pick(own, a, b):
        return jnp.where((own > 0)[None], a, b)

    gain = in_gain_ref[...]
    w_r = jnp.concatenate([w_right_ref[...], w_right_gate_ref[...]], axis=1)
    k_ids = lax.broadcasted_iota(jnp.int32, (tokens, channels), 0)
    valid_v = jnp.full((tokens, channels), valid_ref[0], jnp.int32)
    k_live = k_ids < valid_v

    def normal(rows):
        flat = rows.astype(jnp.float32).reshape(step * tokens, channels)
        return layer_norm(flat, gain).astype(jnp.bfloat16)

    def edge(flat, weights, row_v):
        proj = jnp.dot(flat, weights, preferred_element_type=jnp.float32)
        val = jax.nn.sigmoid(proj[:, channels:]) * proj[:, :channels]
        val = val.reshape(step, tokens, channels)
        out = []
        for r in range(step):
            live = jnp.logical_and(k_live, row_v + r < valid_v)
            rounded = jnp.where(live, val[r], 0.0).astype(jnp.bfloat16)
            out.append(rounded.astype(jnp.float32))
        return out

    w_l = jnp.concatenate([w_left_ref[...], w_left_gate_ref[...]], axis=1)

    def left_chunk(q):
        rows = pl.ds(q * step, step)
        flat = normal(x_ref[rows])
        normed_ref[rows] = flat.reshape(step, tokens, channels)
        row_v = jnp.full((tokens, channels), me * local_rows + q * step, jnp.int32)
        for r, e in enumerate(edge(flat, w_l, row_v)):
            left_ref[q * step + r] = e

    for q in range(CHUNKS):
        left_chunk(q)

    gate_in = normed_ref[:, :width, :]
    for block in range(1, tokens // width):
        at_block = flag(win_v[:width] == block)
        gate_in = pick(at_block, normed_ref[:, block * width : (block + 1) * width, :], gate_in)
    gate_in = gate_in.reshape(local_rows * width, channels)
    gate_vals = jax.nn.sigmoid(
        jnp.dot(gate_in, w_gate_ref[...], preferred_element_type=jnp.float32)
    )

    for q in range(CHUNKS):
        rows = pl.ds(q * step, step)
        held = x_ref[rows, mine]
        for t in range(3):
            copy(QUARTER + t, q).wait_recv()
            held = pick(owners[t], parts[t, rows], held)
        best[rows] = held
        copy(CROSS, q).start()

    for q in range(CHUNKS):
        rows = pl.ds(q * step, step)
        copy(CROSS, q).wait_recv()
        win_ref[core, rows, mine] = pick(own_quad, best[rows], cross[rows])
        for t in range(3):
            copy(GATHER + t, q).start()

    def contract(side, q):
        first = side * local_rows + q * step
        row_v = jnp.full((tokens, channels), win * width + first, jnp.int32)
        flat = normal(win_ref[side, pl.ds(q * step, step)])
        for r, right in enumerate(edge(flat, w_r, row_v)):
            prod_ref[:, pl.ds(first + r, 1), :] = jnp.sum(
                left_ref[...] * right[None], axis=1, keepdims=True
            )

    for q in range(CHUNKS + 1):
        if q < CHUNKS:
            for t in range(3):
                copy(GATHER + t, q).wait_recv()
            copy(SWAP, q).start()
            contract(core, q)
        if q > 0:
            copy(SWAP, q - 1).wait_recv()
            contract(1 - core, q - 1)

    product = prod_ref[...].reshape(local_rows * width, channels)
    normed_out = layer_norm(product, out_gain_ref[...]).astype(jnp.bfloat16)
    result = jnp.dot(normed_out, w_out_ref[...], preferred_element_type=jnp.float32)
    o_ref[...] = (gate_vals * result).astype(jnp.bfloat16).reshape(local_rows, width, channels)

    for q in range(CHUNKS):
        for kind in range(SWAP + 1):
            copy(kind, q).wait_send()


def fused(
    pair_rows, in_gain, w_left, w_left_gate, w_right, w_right_gate, w_gate, w_out, out_gain, valid_len, window
):
    local_rows, tokens, channels = pair_rows.shape
    width = tokens // 8
    vmem = pl.BlockSpec(memory_space=pltpu.VMEM)
    smem = pl.BlockSpec(memory_space=pltpu.SMEM)
    part = (local_rows, tokens // QUAD, channels)
    return pl.pallas_call(
        fused_kernel,
        out_shape=jax.ShapeDtypeStruct((local_rows, width, channels), jnp.bfloat16),
        in_specs=[smem, smem] + [pl.BlockSpec(memory_space=pl.ANY)] * 9,
        out_specs=vmem,
        scratch_shapes=[
            pltpu.VMEM((local_rows, tokens, channels), jnp.bfloat16),
            pltpu.VMEM((1, channels), jnp.float32),
            *[pltpu.VMEM((channels, channels), jnp.bfloat16)] * 6,
            pltpu.VMEM((1, channels), jnp.float32),
            pltpu.VMEM((local_rows, tokens, channels), jnp.bfloat16),
            pltpu.VMEM((local_rows, tokens, channels), jnp.float32),
            pltpu.VMEM((3, *part), jnp.bfloat16),
            pltpu.VMEM(part, jnp.bfloat16),
            pltpu.VMEM(part, jnp.bfloat16),
            pltpu.VMEM((2, local_rows, tokens, channels), jnp.bfloat16),
            pltpu.VMEM((local_rows, width, channels), jnp.float32),
            pltpu.SemaphoreType.DMA((SWAP + 1, CHUNKS)),
            pltpu.SemaphoreType.DMA((SWAP + 1, CHUNKS)),
            pltpu.SemaphoreType.DMA((8 + CHUNKS,)),
        ],
        compiler_params=pltpu.CompilerParams(collective_id=0, has_side_effects=True),
    )(
        valid_len,
        window,
        pair_rows,
        in_gain.reshape(1, channels),
        w_left,
        w_left_gate,
        w_right,
        w_right_gate,
        w_gate,
        w_out,
        out_gain.reshape(1, channels),
    )


def on_device_any(row_devices, pair_rows, *rest):
    local_rows, tokens, channels = pair_rows.shape
    fits = row_devices == QUAD * 4 and tokens // 8 == 2 * local_rows and local_rows % CHUNKS == 0
    return (fused if fits else on_device)(pair_rows, *rest)


def solution(mesh):
    return jax.shard_map(
        functools.partial(on_device_any, mesh.shape["row"]),
        mesh=mesh,
        in_specs=(
            P(("groups", "row"), None, None),
            P(),
            P(),
            P(),
            P(),
            P(),
            P(),
            P(),
            P(),
            P("groups"),
            P("groups"),
        ),
        out_specs=P(("groups", "row"), None, None),
        check_vma=False,
    )
```

profile of v0, /device:TPU:0, one launch (start us, length us, event | category | flops | bytes accessed | tf_op | source)
XLA Modules:
  0.0 22.4 jit_solution(15678620986074373126)
XLA Ops:
  1.3 19.7 %shard_map.109 = bf16[8,16,128]{2,1,0:T(8,128)(2,1)} custom-call(s32[1]{0:T(128)S(6)} %copy.13.valid_ref, s32[1]{0:T(128)S(6)} %copy.14.window_ref, bf16[8,128,128]{2,1,0:T(8,128)(2,1)} %x_hbm.1, f32[1,128]{1,0:T(1,128)} %bitcast.2, bf16[128,128]{1,0:T(8,128)(2,1)} %w_left_hbm.1, bf16[128,128]{1,0:T(8,128)(2,1)} %w_left_gate_hbm.1, ...), custom_call_target="tpu_custom_call" | custom-call | tf_op jit(solution)/shard_map/pallas_call | solution.py:296
  21.0 1.4 %copy.15 = bf16[8,16,128]{2,1,0:T(8,128)(2,1)} copy(bf16[8,16,128]{2,1,0:T(8,128)(2,1)} %shard_map.109) | data formatting | bytes 65536
where the time goes:
time: 22.6 us; the launch traced here: 22.4 us
  Pallas kernels  19.7 us (87%)
  local copies, waits for them, and re-layouts  1.38 us (6%)
  between operations  1.3 us (6%)
    pallas_call x1, Pallas kernels, fused(): pl.pallas_call(fused_kernel, out_shape=jax.ShapeDtypeStruct((local_rows,...  19.7 us
    unnamed x1, local copies, waits for them, and re-layouts  1.38 us

commit v1 on v0

v1 whole, which is shorter than its diff:
```python
import functools

import jax
import jax.numpy as jnp
from jax import lax
from jax.experimental import pallas as pl
from jax.experimental.pallas import tpu as pltpu
from jax.sharding import PartitionSpec as P


def layer_norm(values, gain):
    mean_v = jnp.mean(values, axis=-1, keepdims=True)
    centered = values - mean_v
    variance_v = jnp.mean(centered * centered, axis=-1, keepdims=True)
    return centered * lax.rsqrt(variance_v + 1e-05) * gain


def on_device(
    pair_rows,
    in_gain,
    w_left,
    w_left_gate,
    w_right,
    w_right_gate,
    w_gate,
    w_out,
    out_gain,
    valid_len,
    window,
):
    my_index = lax.axis_index("row")
    local_rows, tokens_all, channels = pair_rows.shape
    width_win = tokens_all // 8
    valid_upto = valid_len[0]
    start_block = window[0]
    start_row = start_block * width_win
    row_ids = my_index * local_rows + jnp.arange(local_rows, dtype=jnp.int32)
    row_live = (row_ids < valid_upto).astype(jnp.float32)
    col_live = (jnp.arange(tokens_all, dtype=jnp.int32) < valid_upto).astype(jnp.float32)
    live_mask = (row_live[:, None] * col_live[None, :])[:, :, None]
    normed = layer_norm(pair_rows.astype(jnp.float32), in_gain).astype(jnp.bfloat16)
    flat_rows = normed.reshape(-1, channels)
    joined = jnp.concatenate([w_left, w_left_gate, w_right, w_right_gate], axis=1)
    projected = jnp.dot(flat_rows, joined, preferred_element_type=jnp.float32)
    projected = projected.reshape(local_rows, tokens_all, 4 * channels)
    left_edge = (
        jax.nn.sigmoid(projected[:, :, channels : 2 * channels])
        * projected[:, :, :channels]
        * live_mask
    ).astype(jnp.bfloat16)
    right_edge = (
        jax.nn.sigmoid(projected[:, :, 3 * channels :])
        * projected[:, :, 2 * channels : 3 * channels]
        * live_mask
    ).astype(jnp.bfloat16)
    gate_in = lax.dynamic_slice_in_dim(normed, start_row, width_win, 1)
    gate_vals = jax.nn.sigmoid(
        jnp.dot(gate_in.reshape(-1, channels), w_gate, preferred_element_type=jnp.float32)
    )
    gate_vals = gate_vals.reshape(local_rows, width_win, channels)
    regrouped = lax.all_to_all(right_edge, "row", split_axis=1, concat_axis=0, tiled=True)
    picked = lax.dynamic_slice_in_dim(regrouped, start_row, width_win, 0)
    window_right = lax.all_gather(picked, "row", axis=1, tiled=True)
    product = jnp.einsum(
        "ikc,jkc->ijc", left_edge, window_right, preferred_element_type=jnp.float32
    )
    normed_out = layer_norm(product, out_gain).astype(jnp.bfloat16)
    result = jnp.dot(normed_out.reshape(-1, channels), w_out, preferred_element_type=jnp.float32)
    return (gate_vals * result.reshape(local_rows, width_win, channels)).astype(jnp.bfloat16)


MESH = pl.DeviceIdType.MESH
CHUNKS = 2
QUAD = 4
PEERS = 3
HOME = PEERS
QUARTER, CROSS, FORWARD, PARTIAL = 0, PEERS, PEERS + 1, 2 * PEERS + 2


def fused_kernel(
    valid_hbm,
    window_hbm,
    x_hbm,
    in_gain_hbm,
    w_left_hbm,
    w_left_gate_hbm,
    w_right_hbm,
    w_right_gate_hbm,
    w_gate_hbm,
    w_out_hbm,
    out_gain_hbm,
    o_ref,
    valid_ref,
    window_ref,
    x_ref,
    in_gain_ref,
    w_l_ref,
    w_r_ref,
    w_gate_ref,
    w_out_ref,
    out_gain_ref,
    parts,
    best,
    cross,
    left_ref,
    right_ref,
    outbox,
    inbox,
    send_sem,
    recv_sem,
    load_sem,
):
    local_rows, tokens, channels = x_ref.shape
    depth = tokens // QUAD
    width = o_ref.shape[1]
    step = local_rows // CHUNKS

    me = lax.axis_index("row")
    core = lax.rem(me, 2)
    chip = lax.div(me, 2)
    quad = lax.div(chip, QUAD)
    spot = lax.rem(chip, QUAD)
    y = lax.rem(spot, 2)
    z = lax.div(spot, 2)
    spots = ((1 - z) * 2 + 1 - y, (1 - z) * 2 + y, z * 2 + 1 - y, spot)

    def at(quad_, spot_, core_):
        return {"row": (quad_ * QUAD + spot_) * 2 + core_}

    cores = (core, 1 - core)
    cross_peer = at(1 - quad, spot, core)
    partner = at(quad, spot, 1 - core)

    def quarter(s):
        return pl.ds(pl.multiple_of(s * depth, depth), depth)

    mine = quarter(spot)

    def remote(src, dst, kind, q, dev):
        return pltpu.make_async_remote_copy(
            src_ref=src,
            dst_ref=dst,
            send_sem=send_sem.at[kind, q],
            recv_sem=recv_sem.at[kind, q],
            device_id=dev,
            device_id_type=MESH,
        )

    def quarter_copy(t, q):
        rows = pl.ds(q * step, step)
        return remote(x_hbm.at[rows, quarter(spots[t])], parts.at[t, 0, rows], QUARTER + t, q, at(quad, spots[t], core))

    def cross_copy(q):
        rows = pl.ds(q * step, step)
        return remote(best.at[rows], cross.at[rows], CROSS, q, cross_peer)

    def forward_copy(t):
        src = x_hbm.at[:, mine] if t == HOME else parts.at[t, 0]
        return remote(src, parts.at[t, 1], FORWARD + t, 0, partner)

    def partial_copy(t, k):
        return remote(outbox.at[t, k], inbox.at[t, k], PARTIAL + t, k, at(quad, spots[t], cores[k]))

    barrier = pltpu.get_barrier_semaphore()
    everyone = [cross_peer] + [at(quad, s, c) for s in spots for c in cores][:-2] + [partner]
    for peer in everyone:
        pl.semaphore_signal(barrier, inc=1, device_id=peer, device_id_type=MESH)
    half = pl.ds(0, channels)
    other = pl.ds(channels, channels)
    loads = [
        pltpu.make_async_copy(src, dst, load_sem.at[n])
        for n, (src, dst) in enumerate(
            (
                (x_hbm.at[:, mine], parts.at[HOME, 0]),
                (valid_hbm, valid_ref),
                (window_hbm, window_ref),
                (in_gain_hbm, in_gain_ref),
                (w_left_hbm, w_l_ref.at[:, half]),
                (w_left_gate_hbm, w_l_ref.at[:, other]),
                (x_hbm, x_ref),
                (w_gate_hbm, w_gate_ref),
                (w_right_hbm, w_r_ref.at[:, half]),
                (w_right_gate_hbm, w_r_ref.at[:, other]),
                (w_out_hbm, w_out_ref),
                (out_gain_hbm, out_gain_ref),
            )
        )
    ]
    for load in loads:
        load.start()
    pl.semaphore_wait(barrier, len(everyone))
    for q in range(CHUNKS):
        for t in range(PEERS):
            quarter_copy(t, q).start()
    forward_copy(HOME).start()
    for load in loads:
        load.wait()

    win = window_ref[0, 0]
    valid = valid_ref[0, 0]
    win_v = jnp.full((depth, channels), win, jnp.int32)

    def flag(cond):
        return jnp.where(cond, 1.0, 0.0).astype(jnp.bfloat16)

    owners = [flag(win_v == quad * QUAD + s) for s in spots[:PEERS]]
    own_quad = flag(jnp.logical_and(win_v >= quad * QUAD, win_v < (quad + 1) * QUAD))

    def pick(own, a, b):
        return jnp.where((own > 0)[None], a, b)

    gain = in_gain_ref[...]
    k_ids = spot * depth + lax.broadcasted_iota(jnp.int32, (depth, channels), 0)
    valid_v = jnp.full((depth, channels), valid, jnp.int32)
    k_live = k_ids < valid_v

    def normal(rows):
        flat = rows.astype(jnp.float32).reshape(-1, channels)
        return layer_norm(flat, gain).astype(jnp.bfloat16)

    def edge(rows, weights, first):
        count = rows.shape[0]
        proj = jnp.dot(normal(rows), weights, preferred_element_type=jnp.float32)
        val = jax.nn.sigmoid(proj[:, channels:]) * proj[:, :channels]
        val = val.reshape(count, depth, channels)
        row_v = jnp.full((depth, channels), first, jnp.int32)
        out = []
        for r in range(count):
            live = jnp.logical_and(k_live, row_v + r < valid_v)
            rounded = jnp.where(live, val[r], 0.0).astype(jnp.bfloat16)
            out.append(rounded.astype(jnp.float32))
        return out

    def left(t, k):
        first = ((quad * QUAD + spots[t]) * 2 + cores[k]) * local_rows
        for r, e in enumerate(edge(parts[t, k], w_l_ref[...], first)):
            left_ref[t, k, r] = e

    gate_in = x_ref[:, :width, :]
    for block in range(1, tokens // width):
        at_block = flag(win_v[:width] == block)
        gate_in = pick(at_block, x_ref[:, block * width : (block + 1) * width, :], gate_in)
    gate_in = normal(gate_in)
    gate_vals = jax.nn.sigmoid(
        jnp.dot(gate_in, w_gate_ref[...], preferred_element_type=jnp.float32)
    )
    left(HOME, 0)

    for q in range(CHUNKS):
        rows = pl.ds(q * step, step)
        held = parts[HOME, 0, rows]
        for t in range(PEERS):
            quarter_copy(t, q).wait_recv()
            held = pick(owners[t], parts[t, 0, rows], held)
        best[rows] = held
        cross_copy(q).start()
    for t in range(PEERS):
        forward_copy(t).start()
    for t in range(PEERS):
        left(t, 0)
    for t in (HOME, *range(PEERS)):
        forward_copy(t).wait_recv()
        left(t, 1)

    for q in range(CHUNKS):
        rows = pl.ds(q * step, step)
        cross_copy(q).wait_recv()
        chosen = pick(own_quad, best[rows], cross[rows])
        first = win * width + core * local_rows + q * step
        for r, e in enumerate(edge(chosen, w_r_ref[...], first)):
            right_ref[:, q * step + r, :] = e

    def contract(t, k):
        sums = [jnp.zeros((local_rows, channels), jnp.float32)] * local_rows
        for d in range(depth):
            right = right_ref[d]
            for r in range(local_rows):
                row = jnp.broadcast_to(left_ref[t, k, r, pl.ds(d, 1), :], (local_rows, channels))
                sums[r] = sums[r] + row * right
        return sums

    for t in range(PEERS + 1):
        for k in (1, 0):
            sums = contract(t, k)
            if (t, k) != (HOME, 0):
                for r in range(local_rows):
                    outbox[t, k, r] = sums[r].astype(jnp.bfloat16)
                partial_copy(t, k).start()

    here = list(sums)
    there = [jnp.zeros((local_rows, channels), jnp.float32)] * local_rows
    for t in range(PEERS + 1):
        for k in (1, 0):
            if (t, k) != (HOME, 0):
                partial_copy(t, k).wait_recv()
                for r in range(local_rows):
                    term = inbox[t, k, r].astype(jnp.float32)
                    if k == 0:
                        here[r] = here[r] + term
                    else:
                        there[r] = there[r] + term
    first_core = jnp.full((local_rows, channels), core, jnp.int32) == 0
    product = jnp.concatenate(
        [
            v
            for r in range(local_rows)
            for v in (jnp.where(first_core, here[r], there[r]), jnp.where(first_core, there[r], here[r]))
        ],
        axis=0,
    )
    normed_out = layer_norm(product, out_gain_ref[...]).astype(jnp.bfloat16)
    result = jnp.dot(normed_out, w_out_ref[...], preferred_element_type=jnp.float32)
    o_ref[...] = (gate_vals * result).astype(jnp.bfloat16).reshape(local_rows, width, channels)

    for q in range(CHUNKS):
        for t in range(PEERS):
            quarter_copy(t, q).wait_send()
        cross_copy(q).wait_send()
    for t in range(PEERS + 1):
        forward_copy(t).wait_send()
        for k in (1, 0):
            if (t, k) != (HOME, 0):
                partial_copy(t, k).wait_send()


def fused(
    pair_rows, in_gain, w_left, w_left_gate, w_right, w_right_gate, w_gate, w_out, out_gain, valid_len, window
):
    local_rows, tokens, channels = pair_rows.shape
    width = tokens // 8
    depth = tokens // QUAD
    part = (local_rows, depth, channels)
    mail = (QUAD, 2, local_rows, local_rows, channels)
    return pl.pallas_call(
        fused_kernel,
        out_shape=jax.ShapeDtypeStruct((local_rows, width, channels), jnp.bfloat16),
        in_specs=[pl.BlockSpec(memory_space=pltpu.HBM)] * 11,
        out_specs=pl.BlockSpec(memory_space=pltpu.VMEM),
        scratch_shapes=[
            pltpu.SMEM((1, 1), jnp.int32),
            pltpu.SMEM((1, 1), jnp.int32),
            pltpu.VMEM((local_rows, tokens, channels), jnp.bfloat16),
            pltpu.VMEM((1, channels), jnp.float32),
            pltpu.VMEM((channels, 2 * channels), jnp.bfloat16),
            pltpu.VMEM((channels, 2 * channels), jnp.bfloat16),
            pltpu.VMEM((channels, channels), jnp.bfloat16),
            pltpu.VMEM((channels, channels), jnp.bfloat16),
            pltpu.VMEM((1, channels), jnp.float32),
            pltpu.VMEM((QUAD, 2, *part), jnp.bfloat16),
            pltpu.VMEM(part, jnp.bfloat16),
            pltpu.VMEM(part, jnp.bfloat16),
            pltpu.VMEM((QUAD, 2, *part), jnp.float32),
            pltpu.VMEM((depth, local_rows, channels), jnp.float32),
            pltpu.VMEM(mail, jnp.bfloat16),
            pltpu.VMEM(mail, jnp.bfloat16),
            pltpu.SemaphoreType.DMA((PARTIAL + QUAD, 2)),
            pltpu.SemaphoreType.DMA((PARTIAL + QUAD, 2)),
            pltpu.SemaphoreType.DMA((12,)),
        ],
        compiler_params=pltpu.CompilerParams(collective_id=0, has_side_effects=True),
    )(
        valid_len.reshape(1, 1),
        window.reshape(1, 1),
        pair_rows,
        in_gain.reshape(1, channels),
        w_left,
        w_left_gate,
        w_right,
        w_right_gate,
        w_gate,
        w_out,
        out_gain.reshape(1, channels),
    )


def on_device_any(row_devices, pair_rows, *rest):
    local_rows, tokens, channels = pair_rows.shape
    fits = row_devices == QUAD * 4 and tokens // 8 == 2 * local_rows and local_rows % CHUNKS == 0
    return (fused if fits else on_device)(pair_rows, *rest)


def solution(mesh):
    return jax.shard_map(
        functools.partial(on_device_any, mesh.shape["row"]),
        mesh=mesh,
        in_specs=(
            P(("groups", "row"), None, None),
            P(),
            P(),
            P(),
            P(),
            P(),
            P(),
            P(),
            P(),
            P("groups"),
            P("groups"),
        ),
        out_specs=P(("groups", "row"), None, None),
        check_vma=False,
    )
```

time: 22.6 us -> 22.1 us (0.978)
  Pallas kernels: 19.7 us -> 19.3 us
    pallas_call x1, Pallas kernels: 19.7 us -> 19.3 us  [fused(): pl.pallas_call(fused_kernel, out_shape=jax.ShapeDtypeStruct((local_rows,...]
where the time goes in v1:
time: 22.1 us; the launch traced here: 22 us
  Pallas kernels  19.3 us (87%)
  local copies, waits for them, and re-layouts  1.38 us (6%)
  between operations  1.3 us (6%)
    pallas_call x1, Pallas kernels, fused(): pl.pallas_call(fused_kernel, out_shape=jax.ShapeDtypeStruct((local_rows,...  19.3 us
    unnamed x1, local copies, waits for them, and re-layouts  1.38 us

profile of v1, /device:TPU:0, one launch (start us, length us, event | category | flops | bytes accessed | tf_op | source)
XLA Modules:
  0.0 22.0 jit_solution(7617775526055216070)
XLA Ops:
  1.3 19.3 %shard_map.109 = bf16[8,16,128]{2,1,0:T(8,128)(2,1)} custom-call(s32[1,1]{1,0:T(1,128)} %bitcast.4.valid_hbm, s32[1,1]{1,0:T(1,128)} %bitcast.5.window_hbm, bf16[8,128,128]{2,1,0:T(8,128)(2,1)} %x_hbm.1, f32[1,128]{1,0:T(1,128)} %bitcast.6, bf16[128,128]{1,0:T(8,128)(2,1)} %w_left_hbm.1, bf16[128,128]{1,0:T(8,128)(2,1)} %w_left_gate_hbm.1, ...), custom_call_target="tpu_custom_call" | custom-call | tf_op jit(solution)/shard_map/pallas_call | solution.py:334
  20.6 1.4 %copy.15 = bf16[8,16,128]{2,1,0:T(8,128)(2,1)} copy(bf16[8,16,128]{2,1,0:T(8,128)(2,1)} %shard_map.109) | data formatting | bytes 65536

commit v2 on v1

--- a/solution.py
+++ b/solution.py
@@ -333,7 +333,7 @@
     mail = (QUAD, 2, local_rows, local_rows, channels)
     return pl.pallas_call(
         fused_kernel,
-        out_shape=jax.ShapeDtypeStruct((local_rows, width, channels), jnp.bfloat16),
+        out_shape=pltpu.VMEM((local_rows, width, channels), jnp.bfloat16),
         in_specs=[pl.BlockSpec(memory_space=pltpu.HBM)] * 11,
         out_specs=pl.BlockSpec(memory_space=pltpu.VMEM),
         scratch_shapes=[

time: 22.1 us -> 20.7 us (0.937)
  local copies, waits for them, and re-layouts: 1.38 us -> 0.62 us
  Pallas kernels: 19.3 us -> 18.7 us
    unnamed x1, local copies, waits for them, and re-layouts: 1.38 us -> 0.62 us
    pallas_call x1, Pallas kernels: 19.3 us -> 18.7 us  [fused(): pl.pallas_call(fused_kernel, out_shape=pltpu.VMEM((local_rows, width, cha...]
where the time goes in v2:
time: 20.7 us; the launch traced here: 20.6 us
  Pallas kernels  18.7 us (90%)
  between operations  1.3 us (6%)
  local copies, waits for them, and re-layouts  0.62 us (3%)
    pallas_call x1, Pallas kernels, fused(): pl.pallas_call(fused_kernel, out_shape=pltpu.VMEM((local_rows, width, cha...  18.7 us
    unnamed x1, local copies, waits for them, and re-layouts  0.62 us

profile of v2, /device:TPU:0, one launch (start us, length us, event | category | flops | bytes accessed | tf_op | source)
XLA Modules:
  0.0 20.6 jit_solution(6302157940488143167)
XLA Ops:
  1.3 18.7 %shard_map.109 = bf16[8,16,128]{2,1,0:T(8,128)(2,1)S(1)} custom-call(s32[1,1]{1,0:T(1,128)} %bitcast.4.valid_hbm, s32[1,1]{1,0:T(1,128)} %bitcast.5.window_hbm, bf16[8,128,128]{2,1,0:T(8,128)(2,1)} %x_hbm.1, f32[1,128]{1,0:T(1,128)} %bitcast.6, bf16[128,128]{1,0:T(8,128)(2,1)} %w_left_hbm.1, bf16[128,128]{1,0:T(8,128)(2,1)} %w_left_gate_hbm.1, ...), custom_call_target="tpu_custom_call" | custom-call | tf_op jit(solution)/shard_map/pallas_call | solution.py:334
  20.0 0.6 %copy.13 = bf16[8,16,128]{2,1,0:T(8,128)(2,1)} copy(bf16[8,16,128]{2,1,0:T(8,128)(2,1)S(1)} %shard_map.109) | data formatting | bytes 65536

commit v3 on v2

--- a/solution.py
+++ b/solution.py
@@ -162,7 +162,7 @@
         return remote(outbox.at[t, k], inbox.at[t, k], PARTIAL + t, k, at(quad, spots[t], cores[k]))
 
     barrier = pltpu.get_barrier_semaphore()
-    everyone = [cross_peer] + [at(quad, s, c) for s in spots for c in cores][:-2] + [partner]
+    everyone = [cross_peer] + [at(quad, s, core) for s in spots[:PEERS]] + [partner]
     for peer in everyone:
         pl.semaphore_signal(barrier, inc=1, device_id=peer, device_id_type=MESH)
     half = pl.ds(0, channels)
@@ -186,12 +186,12 @@
             )
         )
     ]
-    for load in loads:
-        load.start()
     pl.semaphore_wait(barrier, len(everyone))
     for q in range(CHUNKS):
         for t in range(PEERS):
             quarter_copy(t, q).start()
+    for load in loads:
+        load.start()
     forward_copy(HOME).start()
     for load in loads:
         load.wait()
@@ -236,16 +236,6 @@
         for r, e in enumerate(edge(parts[t, k], w_l_ref[...], first)):
             left_ref[t, k, r] = e
 
-    gate_in = x_ref[:, :width, :]
-    for block in range(1, tokens // width):
-        at_block = flag(win_v[:width] == block)
-        gate_in = pick(at_block, x_ref[:, block * width : (block + 1) * width, :], gate_in)
-    gate_in = normal(gate_in)
-    gate_vals = jax.nn.sigmoid(
-        jnp.dot(gate_in, w_gate_ref[...], preferred_element_type=jnp.float32)
-    )
-    left(HOME, 0)
-
     for q in range(CHUNKS):
         rows = pl.ds(q * step, step)
         held = parts[HOME, 0, rows]
@@ -254,6 +244,16 @@
             held = pick(owners[t], parts[t, 0, rows], held)
         best[rows] = held
         cross_copy(q).start()
+    gate_in = x_ref[:, :width, :]
+    for block in range(1, tokens // width):
+        at_block = flag(win_v[:width] == block)
+        gate_in = pick(at_block, x_ref[:, block * width : (block + 1) * width, :], gate_in)
+    gate_in = normal(gate_in)
+    gate_vals = jax.nn.sigmoid(
+        jnp.dot(gate_in, w_gate_ref[...], preferred_element_type=jnp.float32)
+    )
+    left(HOME, 0)
+
     for t in range(PEERS):
         forward_copy(t).start()
     for t in range(PEERS):

time: 20.7 us -> 20.1 us (0.971)
  Pallas kernels: 18.7 us -> 18 us
    pallas_call x1, Pallas kernels: 18.7 us -> 18 us  [fused(): pl.pallas_call(fused_kernel, out_shape=pltpu.VMEM((local_rows, width, cha...]
where the time goes in v3:
time: 20.1 us; the launch traced here: 19.9 us
  Pallas kernels  18 us (90%)
  between operations  1.3 us (6%)
  local copies, waits for them, and re-layouts  0.62 us (3%)
    pallas_call x1, Pallas kernels, fused(): pl.pallas_call(fused_kernel, out_shape=pltpu.VMEM((local_rows, width, cha...  18 us
    unnamed x1, local copies, waits for them, and re-layouts  0.62 us

profile of v3, /device:TPU:0, one launch (start us, length us, event | category | flops | bytes accessed | tf_op | source)
XLA Modules:
  0.0 19.9 jit_solution(11316826141090218617)
XLA Ops:
  1.3 18.0 %shard_map.109 = bf16[8,16,128]{2,1,0:T(8,128)(2,1)S(1)} custom-call(s32[1,1]{1,0:T(1,128)} %bitcast.4.valid_hbm, s32[1,1]{1,0:T(1,128)} %bitcast.5.window_hbm, bf16[8,128,128]{2,1,0:T(8,128)(2,1)} %x_hbm.1, f32[1,128]{1,0:T(1,128)} %bitcast.6, bf16[128,128]{1,0:T(8,128)(2,1)} %w_left_hbm.1, bf16[128,128]{1,0:T(8,128)(2,1)} %w_left_gate_hbm.1, ...), custom_call_target="tpu_custom_call" | custom-call | tf_op jit(solution)/shard_map/pallas_call | solution.py:334
  19.3 0.6 %copy.13 = bf16[8,16,128]{2,1,0:T(8,128)(2,1)} copy(bf16[8,16,128]{2,1,0:T(8,128)(2,1)S(1)} %shard_map.109) | data formatting | bytes 65536
